TPU v7x, 512 devices: a whole 4x8x8 slice. The times are simulated.
512 devices in a mesh: ctx: 32 (over y, z_lo), head: 4 (over x), batch: 4 (over z_hi, core).
Axes of the slice: x: 4, y: 8, z: 8 (z_hi: 2, z_lo: 4; z = z_hi * 4 + z_lo), core: 2. Of those that a mesh axis runs over, the one named last changes fastest.
Arguments:
- queries: bfloat16 [4, 4096, 20, 128], P('batch', 'ctx', 'head'), may hold values from -64 to 64
- key_rows: bfloat16 [4, 4096, 4, 128], P('batch', 'ctx', 'head'), may hold values from -8 to 8
- block_order: int32 [64], replicated, may hold values from 0 to 63, each once
- conv_len: int32 [4], replicated, may hold values from 2048 to 4096
- gate_wq: float32 [128, 128], replicated, may hold values from -32 to 32
- gate_wk: float32 [384, 128], replicated, may hold values from -32 to 32
Outputs:
- teacher_map: float32 [4, 20, 64, 64], P('batch', 'head', 'ctx')
- grad_wq: float32 [128, 128], replicated
- grad_wk: float32 [384, 128], replicated
All inputs are finite; a program needn't handle non-finite values.
Results may differ from a plain program's by a relative error of at most 0.0003.
Values may be sent and summed in bfloat16 or wider, within the bound.
No kernel may reach another device: no remote copies, remote signals or barrier semaphores. Data moves between devices by JAX's collectives and lax.ppermute only.
A program may use at most 64 MiB of HBM per device.

v0:
```python
import math
import jax
import jax.numpy as jnp
from jax import lax
from jax.sharding import PartitionSpec as P

BLK = 64
masked_value = -1e30
norm_epsilon = 1e-06


def score_tile(query_group, key_tile, query_pos, key_pos, length):
    scores = jnp.einsum(
        "rgqd,kgd->gqrk", query_group, key_tile, preferred_element_type=jnp.float32
    ) / math.sqrt(key_tile.shape[-1])
    allowed = (key_pos[None, :] <= query_pos[:, None]) & (key_pos[None, :] < length)
    return (jnp.where(allowed, scores, masked_value), allowed)


def gate_loss(
    weight_query, weight_key, pooled_query, pooled_key, target_map, query_starts, key_starts, length
):
    kv_heads = pooled_key.shape[1]
    group_size = pooled_query.shape[1] // kv_heads
    width_gate = weight_query.shape[1]
    proj_query = jnp.einsum(
        "bhd,de->bhe", pooled_query, weight_query, precision=lax.Precision.HIGHEST
    )
    proj_key = jnp.einsum("bgd,de->bge", pooled_key, weight_key, precision=lax.Precision.HIGHEST)
    unit_query = proj_query * lax.rsqrt(
        jnp.mean(proj_query * proj_query, axis=-1, keepdims=True) + norm_epsilon
    )
    unit_key = proj_key * lax.rsqrt(
        jnp.mean(proj_key * proj_key, axis=-1, keepdims=True) + norm_epsilon
    )
    query_count = unit_query.shape[0]
    unit_query = unit_query.reshape(query_count, kv_heads, group_size, width_gate)
    logits = jnp.einsum(
        "igqe,jge->gqij", unit_query, unit_key, precision=lax.Precision.HIGHEST
    ) / math.sqrt(width_gate)
    logits = logits.reshape(kv_heads * group_size, query_count, unit_key.shape[0])
    allowed = (key_starts[None, :] <= query_starts[:, None]) & (key_starts[None, :] < length)
    weights_exp = jnp.where(allowed[None], jnp.exp(logits), 0.0)
    log_norm = jnp.log(jnp.sum(weights_exp, axis=-1, keepdims=True))
    positive = target_map > 0
    entropy_part = jnp.where(
        positive, target_map * jnp.log(jnp.where(positive, target_map, 1.0)), 0.0
    )
    divergence = entropy_part - target_map * (logits - log_norm)
    return jnp.sum(divergence)


def body(queries, key_rows, block_order, conv_len, gate_wq, gate_wk):
    tok_dev = queries.shape[1]
    head_dev = queries.shape[2]
    kv_dev = key_rows.shape[2]
    head_size = queries.shape[3]
    group_size = head_dev // kv_dev
    block_dev = tok_dev // BLK
    block_count = block_order.shape[0]
    ctx_index = lax.axis_index("ctx")
    length = lax.dynamic_index_in_dim(conv_len, lax.axis_index("batch"), keepdims=False)
    own_blocks = lax.dynamic_slice_in_dim(block_order, ctx_index * block_dev, block_dev)
    offsets = jnp.arange(BLK, dtype=jnp.int32)
    query_pos = (own_blocks[:, None] * BLK + offsets[None, :]).reshape(tok_dev)
    valid_row = (query_pos < length)[:, None]
    query_group = queries[0].reshape(tok_dev, kv_dev, group_size, head_size)

    def tile_loop(update, carry, segment):
        width_keys = segment.shape[1]
        sub_rows = math.gcd(width_keys, 512)
        key_pos = (block_order[:, None] * BLK + offsets[None, :]).reshape(width_keys)

        def advance(step_index, state):
            first = step_index * sub_rows
            key_tile = lax.dynamic_slice_in_dim(segment[0], first, sub_rows, 0)
            tile_pos = lax.dynamic_slice_in_dim(key_pos, first, sub_rows, 0)
            column = first // BLK
            result = update(state, key_tile, tile_pos, column)
            return result

        return lax.fori_loop(0, width_keys // sub_rows, advance, carry)

    def merge_stats(highest, summed, masked, allowed):
        new_high = jnp.maximum(highest, jnp.max(masked, axis=-1))
        fresh = jnp.sum(jnp.where(allowed, jnp.exp(masked - new_high[..., None]), 0.0), axis=-1)
        return (new_high, summed * jnp.exp(highest - new_high) + fresh)

    stats_shape = (kv_dev, group_size, tok_dev)
    start_high = jnp.full(stats_shape, masked_value, jnp.float32)
    start_sum = jnp.zeros(stats_shape, jnp.float32)

    def add_stats(state, key_tile, tile_pos, column):
        masked, allowed = score_tile(query_group, key_tile, query_pos, tile_pos, length)
        return merge_stats(state[0], state[1], masked, allowed)

    highest, summed = tile_loop(
        add_stats, (start_high, start_sum), lax.all_gather(key_rows, "ctx", axis=1, tiled=True)
    )
    log_total = highest + jnp.log(summed)

    def add_pool(state, key_tile, tile_pos, column):
        masked, allowed = score_tile(query_group, key_tile, query_pos, tile_pos, length)
        probs = jnp.where(valid_row, jnp.exp(masked - log_total[..., None]), 0.0)
        tile_max = probs.reshape(
            kv_dev, group_size, block_dev, BLK, key_tile.shape[0] // BLK, BLK
        ).max(axis=(3, 5))
        return lax.dynamic_update_slice_in_dim(state, tile_max, column, 3)

    start_pool = jnp.zeros((kv_dev, group_size, block_dev, block_count), jnp.float32)
    pooled = tile_loop(add_pool, start_pool, lax.all_gather(key_rows, "ctx", axis=1, tiled=True))
    pooled = pooled.reshape(head_dev, block_dev, block_count)
    query_starts = own_blocks * BLK
    valid_block = (query_starts < length)[None, :, None]
    totals = jnp.sum(pooled, axis=-1, keepdims=True)
    target = jnp.where(valid_block, pooled / jnp.where(valid_block, totals, 1.0), 0.0)
    key_local = key_rows[0].reshape(block_dev, BLK, kv_dev, head_size)
    pooled_local = jnp.concatenate(
        [
            jnp.max(key_local, axis=1).astype(jnp.float32),
            jnp.min(key_local, axis=1).astype(jnp.float32),
            jnp.mean(key_local, axis=1, dtype=jnp.float32),
        ],
        axis=-1,
    )
    pooled_all = lax.all_gather(pooled_local, "ctx", axis=0, tiled=True)
    pooled_query = jnp.mean(
        queries[0].reshape(block_dev, BLK, head_dev, head_size), axis=1, dtype=jnp.float32
    )
    key_starts = block_order * BLK

    def local_loss(weight_query, weight_key):
        return gate_loss(
            weight_query,
            weight_key,
            pooled_query,
            pooled_all,
            target,
            query_starts,
            key_starts,
            length,
        )

    loss_value, pullback = jax.vjp(local_loss, gate_wq, gate_wk)
    grad_query, grad_key = pullback(jnp.ones((), jnp.float32))
    grad_query, grad_key = lax.psum((grad_query, grad_key), ("ctx", "head", "batch"))
    return (target[None], grad_query, grad_key)


def solution(mesh):
    in_specs = (
        P("batch", "ctx", "head", None),
        P("batch", "ctx", "head", None),
        P(),
        P(),
        P(),
        P(),
    )
    out_specs = (P("batch", "head", "ctx", None), P(), P())
    return jax.shard_map(body, mesh=mesh, in_specs=in_specs, out_specs=out_specs, check_vma=False)
```

profile of v0, /device:TPU:23, one launch (start us, length us, event | category | flops | bytes accessed | tf_op | source)
XLA Modules:
  0.0 550.4 jit_solution(3898082681139945655)
XLA Ops:
  10.4 56.8 %all_gather.8 = f32[64,1,384]{2,1,0:T(1,128)S(1)} all-gather(f32[2,1,384]{2,1,0:T(1,128)S(1)} %pad_maximum_fusion), channel_id=1, replica_groups=mesh['ctx'=32,'head'=4,'batch'=4] {'ctx'}, dimensions={0}, use_global_device_ids=true | all-gather | bytes 101376 | tf_op jit(solution)/shard_map/all_gather | solution.py:126
  68.4 1.4 broadcast_compare_fusion.4
  74.0 63.9 %all-gather.2.cloned.1.call-done = bf16[1,4096,1,128]{3,1,2,0:T(8,128)(2,1)} async-done(((bf16[1,128,1,128]{3,1,2,0:T(8,128)(2,1)}), bf16[1,4096,1,128]{3,1,2,0:T(8,128)(2,1)}) %all-gather.2.cloned.1.call-update) | async-done | bytes 1048592 | tf_op jit(solution)/shard_map/all_gather | solution.py:111
  137.8 22.0 %while.33 = (s32[]{:T(128)}, f32[1,5,128]{2,1,0:T(8,128)S(1)}, f32[1,5,128]{2,1,0:T(8,128)S(1)}, s32[4096]{0:T(1024)S(1)}, s32[]{:T(128)}, /*index=5*/bf16[1,409...) while((s32[]{:T(128)}, f32[1,5,128]{2,1,0:T(8,128)S(1)}, ...), condition=%wide.region_3.4_spmd.clone, body=%wide.region_0.3_spmd.clone.sunk | while | flops 85987080 | bytes 3155650 | solution.py:82
  138.9 1.3 fusion.74
  141.7 1.3 fusion.74
  144.4 1.3 fusion.74
  147.2 1.3 fusion.74
  149.9 1.3 fusion.74
  152.7 1.3 fusion.74
  155.4 1.3 fusion.74
  158.2 1.3 fusion.74
  159.9 74.3 %while.34 = (s32[]{:T(128)}, f32[1,5,2,64]{3,2,1,0:T(2,128)S(1)}, s32[4096]{0:T(1024)S(1)}, s32[]{:T(128)}, bf16[1,4096,1,128]{3,1,2,0:T(8,128)(2,1)}, /*index=5...) while((s32[]{:T(128)}, f32[1,5,2,64]{3,2,1,0:T(2,128)S(1)}, ...), condition=%wide.region_6.7_spmd.clone.clone, body=%wide.region_4.6_spmd.clone.clone.sunk | while | flops 85656376 | bytes 5683170 | solution.py:82
  161.8 2.5 exponential_select_fusion.2
  164.3 2.8 reshape.363
  170.5 2.5 exponential_select_fusion.2
  173.0 2.8 reshape.363
  179.9 2.5 exponential_select_fusion.2
  182.4 2.8 reshape.363
  189.3 2.5 exponential_select_fusion.2
  191.8 2.8 reshape.363
  198.6 2.5 exponential_select_fusion.2
  201.1 2.8 reshape.363
  208.0 2.5 exponential_select_fusion.2
  210.5 2.8 reshape.363
  217.4 2.5 exponential_select_fusion.2
  219.9 2.8 reshape.363
  226.8 2.5 exponential_select_fusion.2
  229.3 2.8 reshape.363
  238.2 302.2 %all-reduce.3.cloned.1.call-done = (f32[128,128]{1,0:T(8,128)}, f32[384,128]{1,0:T(8,128)}) async-done(((f32[128,128]{1,0:T(8,128)}, f32[384,128]{1,0:T(8,128)}), (f32[128,128]{1,0:T(8,128)}, f32[384,128]{1,0:T(8,128)})) %all-reduce.3.cloned.1.call-update) | async-done | bytes 262160 | tf_op jit(solution)/shard_map/psum | solution.py:146
  540.4 1.5 copy.90
  541.9 1.6 copy.91
  (178 shorter events, 54.5 us)
Async XLA Ops:
  7.2 64.9 %copy-start = (f32[384,128]{1,0:T(8,128)S(1)}, f32[384,128]{1,0:T(8,128)}, u32[]{:S(2)}) copy-start(f32[384,128]{1,0:T(8,128)} %param.15) | copy-start | bytes 589828
  7.2 130.7 %all-gather.2.cloned.1.call-start = ((), (), s32[]{:S(2)}) async-start(), calls=%async_computation | async-start | bytes 1081344 | tf_op jit(solution)/shard_map/all_gather | solution.py:111
  7.9 532.5 %all-reduce.3.cloned.1.call-start = ((), (), s32[]{:S(2)}) async-start(), calls=%async_computation.1 | async-start | bytes 524288 | tf_op jit(solution)/shard_map/psum | solution.py:146
Sparse Core Ops, SparseCore 0:
  10.1 127.7 all-gather.1
  237.7 302.7 all-reduce.2
where the time goes:
time: 552 us; the launch traced here: 550 us
  waiting for transfers between devices  367 us (66%)
  blocking collectives  56.8 us (10%)
  other arithmetic  39.2 us (7%)
  local copies, waits for them, and re-layouts  36.8 us (7%)
  matrix products  35.6 us (6%)
  between operations  14.1 us (3%)
    psum x1, waiting for transfers between devices, body(): lax.psum((grad_query, grad_key), ('ctx', 'head', 'batch'))  302 us
    all_gather x1, waiting for transfers between devices, body(): lax.all_gather(key_rows, 'ctx', axis=1, tiled=True)  63.9 us
    all_gather x1, blocking collectives, body(): pooled_all = lax.all_gather(pooled_local, 'ctx', axis=0, tiled=True)  56.8 us
    dot_general x16, matrix products, score_tile(): jnp.einsum('rgqd,kgd->gqrk', query_group, key_tile, preferred_element_typ...  30.9 us
    reshape x8, local copies, waits for them, and re-layouts, add_pool(): probs.reshape(kv_dev, group_size, block_dev, BLK, key_tile.shape[0] // BL...  22.6 us
    lt x16, other arithmetic, score_tile(): key_pos[None, :] < length  11.6 us
  transfers between devices with their start and end apart: 2, of which 2 were waited for; matrix products, arithmetic and copies ran while one was open for 2% of the time, Pallas kernels for 0%

commit v1 on v0

--- a/solution.py
+++ b/solution.py
@@ -143,7 +143,7 @@
 
     loss_value, pullback = jax.vjp(local_loss, gate_wq, gate_wk)
     grad_query, grad_key = pullback(jnp.ones((), jnp.float32))
-    grad_query, grad_key = lax.psum((grad_query, grad_key), ("ctx", "head", "batch"))
+    grad_query, grad_key = lax.psum(lax.psum((grad_query, grad_key), ("head", "batch")), "ctx")
     return (target[None], grad_query, grad_key)
 
 

time: 552 us -> 777 us (1.41)
  the two profiles are of different devices: /device:TPU:23 before, /device:TPU:2 now
where the time goes in v1:
time: 777 us; the launch traced here: 776 us
  waiting for transfers between devices  567 us (73%)
  blocking collectives  82.2 us (11%)
  other arithmetic  39.2 us (5%)
  local copies, waits for them, and re-layouts  36.8 us (5%)
  matrix products  35.6 us (5%)
  between operations  13.9 us (2%)
    psum x1, waiting for transfers between devices, body(): lax.psum(lax.psum((grad_query, grad_key), ('head', 'batch')), 'ctx')  323 us
    psum x1, waiting for transfers between devices, body(): lax.psum((grad_query, grad_key), ('head', 'batch'))  176 us
    all_gather x1, blocking collectives, body(): pooled_all = lax.all_gather(pooled_local, 'ctx', axis=0, tiled=True)  82.2 us
    all_gather x1, waiting for transfers between devices, body(): lax.all_gather(key_rows, 'ctx', axis=1, tiled=True)  67.4 us
    dot_general x16, matrix products, score_tile(): jnp.einsum('rgqd,kgd->gqrk', query_group, key_tile, preferred_element_typ...  30.9 us
    reshape x8, local copies, waits for them, and re-layouts, add_pool(): probs.reshape(kv_dev, group_size, block_dev, BLK, key_tile.shape[0] // BL...  22.6 us
  transfers between devices with their start and end apart: 3, of which 3 were waited for; matrix products, arithmetic and copies ran while one was open for 1% of the time, Pallas kernels for 0%

profile of v1, /device:TPU:2, one launch (start us, length us, event | category | flops | bytes accessed | tf_op | source)
XLA Modules:
  0.0 775.8 jit_solution(8161737965345124556)
XLA Ops:
  10.4 82.2 %all_gather.8 = f32[64,1,384]{2,1,0:T(1,128)S(1)} all-gather(f32[2,1,384]{2,1,0:T(1,128)S(1)} %pad_maximum_fusion), channel_id=1, replica_groups=mesh['ctx'=32,'head'=4,'batch'=4] {'ctx'}, dimensions={0}, use_global_device_ids=true | all-gather | bytes 101376 | tf_op jit(solution)/shard_map/all_gather | solution.py:126
  93.9 1.4 broadcast_compare_fusion.4
  99.4 67.4 %all-gather.2.cloned.1.call-done = bf16[1,4096,1,128]{3,1,2,0:T(8,128)(2,1)} async-done(((bf16[1,128,1,128]{3,1,2,0:T(8,128)(2,1)}), bf16[1,4096,1,128]{3,1,2,0:T(8,128)(2,1)}) %all-gather.2.cloned.1.call-update) | async-done | bytes 1048592 | tf_op jit(solution)/shard_map/all_gather | solution.py:111
  166.8 22.0 %while.33 = (s32[]{:T(128)}, f32[1,5,128]{2,1,0:T(8,128)S(1)}, f32[1,5,128]{2,1,0:T(8,128)S(1)}, s32[4096]{0:T(1024)S(1)}, s32[]{:T(128)}, /*index=5*/bf16[1,409...) while((s32[]{:T(128)}, f32[1,5,128]{2,1,0:T(8,128)S(1)}, ...), condition=%wide.region_3.4_spmd.clone, body=%wide.region_0.3_spmd.clone.sunk | while | flops 85987080 | bytes 3155650 | solution.py:82
  170.7 1.3 fusion.74
  173.4 1.3 fusion.74
  176.2 1.3 fusion.74
  178.9 1.3 fusion.74
  181.7 1.3 fusion.74
  184.4 1.3 fusion.74
  187.2 1.3 fusion.74
  188.9 74.3 %while.34 = (s32[]{:T(128)}, f32[1,5,2,64]{3,2,1,0:T(2,128)S(1)}, s32[4096]{0:T(1024)S(1)}, s32[]{:T(128)}, bf16[1,4096,1,128]{3,1,2,0:T(8,128)(2,1)}, /*index=5...) while((s32[]{:T(128)}, f32[1,5,2,64]{3,2,1,0:T(2,128)S(1)}, ...), condition=%wide.region_6.7_spmd.clone.clone, body=%wide.region_4.6_spmd.clone.clone.sunk | while | flops 85656376 | bytes 5683170 | solution.py:82
  190.8 2.5 exponential_select_fusion.2
  193.3 2.8 reshape.363
  199.5 2.5 exponential_select_fusion.2
  202.0 2.8 reshape.363
  208.9 2.5 exponential_select_fusion.2
  211.4 2.8 reshape.363
  218.2 2.5 exponential_select_fusion.2
  220.8 2.8 reshape.363
  227.6 2.5 exponential_select_fusion.2
  230.1 2.8 reshape.363
  237.0 2.5 exponential_select_fusion.2
  239.5 2.8 reshape.363
  246.4 2.5 exponential_select_fusion.2
  248.9 2.8 reshape.363
  255.8 2.5 exponential_select_fusion.2
  258.3 2.8 reshape.363
  266.6 175.9 %all-reduce.7.cloned.1.call-done = (f32[128,128]{1,0:T(8,128)}, f32[384,128]{1,0:T(8,128)}) async-done(((f32[128,128]{1,0:T(8,128)}, f32[384,128]{1,0:T(8,128)}), (f32[128,128]{1,0:T(8,128)}, f32[384,128]{1,0:T(8,128)})) %all-reduce.7.cloned.1.call-update) | async-done | bytes 262160 | tf_op jit(solution)/shard_map/psum | solution.py:146
  443.2 323.0 %all-reduce.5.cloned.1.call-done = (f32[128,128]{1,0:T(8,128)}, f32[384,128]{1,0:T(8,128)}) async-done(((f32[128,128]{1,0:T(8,128)}, f32[384,128]{1,0:T(8,128)}), (f32[128,128]{1,0:T(8,128)}, f32[384,128]{1,0:T(8,128)})) %all-reduce.5.cloned.1.call-update) | async-done | bytes 262160 | tf_op jit(solution)/shard_map/psum | solution.py:146
  766.2 1.5 copy.92
  767.7 1.6 copy.93
  (181 shorter events, 55.9 us)
Async XLA Ops:
  7.2 90.3 %copy-start = (f32[384,128]{1,0:T(8,128)S(1)}, f32[384,128]{1,0:T(8,128)}, u32[]{:S(2)}) copy-start(f32[384,128]{1,0:T(8,128)} %param.15) | copy-start | bytes 589828
  7.2 159.7 %all-gather.2.cloned.1.call-start = ((), (), s32[]{:S(2)}) async-start(), calls=%async_computation | async-start | bytes 1081344 | tf_op jit(solution)/shard_map/all_gather | solution.py:111
  7.9 434.6 %all-reduce.7.cloned.1.call-start = ((), (), s32[]{:S(2)}) async-start(), calls=%async_computation.2 | async-start | bytes 524288 | tf_op jit(solution)/shard_map/psum | solution.py:146
  266.6 499.6 %all-reduce.5.cloned.1.call-start = ((), (), s32[]{:S(2)}) async-start(), calls=%async_computation.1 | async-start | bytes 524288 | tf_op jit(solution)/shard_map/psum | solution.py:146
Sparse Core Ops, SparseCore 0:
  10.1 156.7 all-gather.1
  266.7 175.7 all-reduce.6
  445.4 320.7 all-reduce.4
